TPU v7x, 32 devices: a whole 2x2x4 slice. The times are simulated.
32 devices in a mesh: req: 4 (over z), head: 8 (over y, x, core).
Axes of the slice: x: 2, y: 2, z: 4, core: 2. Of those that a mesh axis runs over, the one named last changes fastest.
Arguments:
- hidden_in: bfloat16 [64, 1024], P(('req', 'head')), may hold values from -6 to 6
- lengths: int32 [64], P('req'), may hold values from 2 to 1024, as said below
- request_order: int32 [64], replicated, may hold values from 0 to 63, each once
- key_cache: bfloat16 [2, 64, 16, 64, 1024], P(None, 'req', 'head')
- value_cache: bfloat16 [2, 64, 16, 64, 1024], P(None, 'req', 'head'), may hold values from -6 to 6
- w_qkv: bfloat16 [2, 16, 1024, 192], P(None, 'head'), may hold values from -0.1875 to 0.1875
- w_out: bfloat16 [2, 16, 64, 1024], P(None, 'head'), may hold values from -0.1875 to 0.1875
- w_up: bfloat16 [2, 1024, 4096], P(None, None, ('req', 'head')), may hold values from -0.1875 to 0.1875
- bias_up: bfloat16 [2, 4096], P(None, ('req', 'head')), may hold values from -3 to 3
- w_down: bfloat16 [2, 1024, 4096], P(None, None, ('req', 'head')), may hold values from -0.09375 to 0.09375
- norm_gain: float32 [2, 2, 1024], replicated, may hold values from 0.1 to 1.9
- norm_bias: float32 [2, 2, 1024], replicated, may hold values from -3 to 3
- embedding: bfloat16 [49152, 1024], P(('req', 'head')), may hold values from -0.59765625 to 0.59765625
Outputs:
- logits: float32 [64, 49152], P(None, ('req', 'head'))
Inputs may be any that keep to these rules, and one draw needn't show every extreme that they name: `lengths`: the largest length is 1024. Slot s of the caches and of lengths belongs to request request_order[s]; each request once.
All inputs are finite; a program needn't handle non-finite values.
Results may differ from a plain program's by a relative error of at most 0.0095.
Values may be sent and summed in bfloat16 or wider, within the bound.
A program may use at most 64 MiB of HBM per device.

v0:
```python
import jax
import jax.numpy as jnp
from jax import lax
from jax.sharding import PartitionSpec as P

LAYERS = 2


def layer_norm(values, gain_vec, bias_vec):
    average = jnp.mean(values, axis=-1, keepdims=True)
    centred = values - average
    variance = jnp.mean(centred * centred, axis=-1, keepdims=True)
    return centred * lax.rsqrt(variance + 1e-05) * gain_vec + bias_vec


def body(
    hidden_in,
    lengths,
    request_order,
    key_cache,
    value_cache,
    w_qkv,
    w_out,
    w_up,
    bias_up,
    w_down,
    norm_gain,
    norm_bias,
    embedding,
):
    group_size = lengths.shape[0]
    row_share = hidden_in.shape[0]
    head_size = w_out.shape[2]
    score_scale = head_size ** (-0.5)
    positions = jnp.arange(key_cache.shape[-1], dtype=jnp.int32)
    valid = positions[None, None, :] < lengths[:, None, None]
    gathered = lax.all_gather(hidden_in, ("req", "head"), axis=0, tiled=True)
    slot_ids = lax.dynamic_slice_in_dim(
        request_order, lax.axis_index("req") * group_size, group_size, 0
    )
    group_rows = gathered[slot_ids]
    own_rows = lax.dynamic_slice_in_dim(
        group_rows, lax.axis_index("head") * row_share, row_share, 0
    )
    for layer_idx in range(LAYERS):
        if layer_idx > 0:
            group_rows = lax.all_gather(own_rows, "head", axis=0, tiled=True)
        projected = jnp.einsum(
            "rd,hde->rhe", group_rows, w_qkv[layer_idx], preferred_element_type=jnp.float32
        ).astype(jnp.bfloat16)
        query = projected[..., :head_size]
        own_key = projected[..., head_size : 2 * head_size]
        own_value = projected[..., 2 * head_size :]
        scores = (
            jnp.einsum(
                "rhd,rhdl->rhl", query, key_cache[layer_idx], preferred_element_type=jnp.float32
            )
            * score_scale
        )
        scores = jnp.where(valid, scores, -jnp.inf)
        own = (
            jnp.sum(query.astype(jnp.float32) * own_key.astype(jnp.float32), axis=-1) * score_scale
        )
        row_max = jnp.maximum(jnp.max(scores, axis=-1), own)
        expo = jnp.exp(scores - row_max[..., None])
        own_exp = jnp.exp(own - row_max)
        denom = jnp.sum(expo, axis=-1) + own_exp
        mixed = jnp.einsum(
            "rhl,rhdl->rhd",
            expo.astype(jnp.bfloat16),
            value_cache[layer_idx],
            preferred_element_type=jnp.float32,
        )
        mixed = mixed + own_exp.astype(jnp.bfloat16).astype(jnp.float32)[
            ..., None
        ] * own_value.astype(jnp.float32)
        head_out = (mixed / denom[..., None]).astype(jnp.bfloat16)
        out_weight = w_out[layer_idx]
        attn_out = lax.psum_scatter(
            jnp.einsum("rhd,hde->re", head_out, out_weight, preferred_element_type=jnp.float32),
            "head",
            scatter_dimension=0,
            tiled=True,
        )
        normed = layer_norm(
            own_rows.astype(jnp.float32) + attn_out,
            norm_gain[layer_idx, 0],
            norm_bias[layer_idx, 0],
        ).astype(jnp.bfloat16)
        up_local = w_up[layer_idx]
        bias_local = bias_up[layer_idx].astype(jnp.float32)
        down_local = w_down[layer_idx]
        pre_act = (
            jnp.dot(
                lax.all_gather(normed, ("req", "head"), axis=0, tiled=True),
                up_local,
                preferred_element_type=jnp.float32,
            )
            + bias_local
        )
        hidden = jax.nn.gelu(pre_act, approximate=False).astype(jnp.bfloat16)
        mlp_out = lax.psum_scatter(
            jnp.einsum("rf,df->rd", hidden, down_local, preferred_element_type=jnp.float32),
            ("req", "head"),
            scatter_dimension=0,
            tiled=True,
        )
        own_rows = layer_norm(
            normed.astype(jnp.float32) + mlp_out, norm_gain[layer_idx, 1], norm_bias[layer_idx, 1]
        ).astype(jnp.bfloat16)
    everything = lax.all_gather(own_rows, ("req", "head"), axis=0, tiled=True)
    inverse = (
        jnp.zeros_like(request_order)
        .at[request_order]
        .set(jnp.arange(request_order.shape[0], dtype=jnp.int32))
    )
    return jnp.dot(everything[inverse], embedding.T, preferred_element_type=jnp.float32)


def solution(mesh):
    placed = (
        P(("req", "head"), None),
        P("req"),
        P(),
        P(None, "req", "head", None, None),
        P(None, "req", "head", None, None),
        P(None, "head", None, None),
        P(None, "head", None, None),
        P(None, None, ("req", "head")),
        P(None, ("req", "head")),
        P(None, None, ("req", "head")),
        P(),
        P(),
        P(("req", "head"), None),
    )
    return jax.shard_map(
        body, mesh=mesh, in_specs=placed, out_specs=P(None, ("req", "head")), check_vma=False
    )
```

profile of v0, /device:TPU:0, one launch (start us, length us, event | category | flops | bytes accessed | tf_op | source)
XLA Modules:
  0.0 567.9 jit_solution(7226839117564876502)
XLA Ops:
  6.5 0.9 compare_select_fusion.2
  7.4 43.9 %all-gather = bf16[32,2,1024]{2,1,0:T(2,128)(2,1)S(1)} all-gather(bf16[1,2,1024]{2,1,0:T(2,128)(2,1)} %bitcast.134), channel_id=1, replica_groups=mesh['req'=4,'head'=8] {'req','head'}, dimensions={0}, use_global_device_ids=true | all-gather | bytes 135168 | tf_op jit(solution)/shard_map/all_gather | solution.py:37
  52.0 1.5 convolution_convert_fusion.1
  54.4 2.9 fusion.6
  57.7 3.4 fusion.4
  61.0 0.9 convolution_bitcast_fusion.1
  63.4 47.4 %all-reduce.9.cloned.1.call-done = f32[16,1024]{1,0:T(8,128)} async-done(((f32[16,1024]{1,0:T(8,128)}), f32[16,1024]{1,0:T(8,128)}) %all-reduce.9.cloned.1.call-update) | async-done | bytes 65552
  110.8 0.9 fusion.215
  111.7 1.0 multiply_reduce_fusion.5
  112.6 0.8 add_convert_fusion.3
  113.5 40.2 %all-gather.1 = bf16[32,2,1024]{2,1,0:T(2,128)(2,1)S(1)} all-gather(bf16[1,2,1024]{2,1,0:T(2,128)(2,1)S(1)} %bitcast.125), channel_id=1, replica_groups=mesh['req'=4,'head'=8] {'req','head'}, dimensions={0}, use_global_device_ids=true | all-gather | bytes 135168 | tf_op jit(solution)/shard_map/all_gather | solution.py:95
  153.8 2.1 fusion.20
  156.0 121.3 %all-reduce.11.cloned.1.call-done = f32[64,1024]{1,0:T(8,128)} async-done(((f32[64,1024]{1,0:T(8,128)}), f32[64,1024]{1,0:T(8,128)}) %all-reduce.11.cloned.1.call-update) | async-done | bytes 262160
  277.3 0.9 fusion.212
  278.2 0.9 multiply_reduce_fusion.4
  279.1 0.8 add_convert_fusion.2
  280.0 9.0 %all-gather.2 = bf16[8,2,1024]{2,1,0:T(2,128)(2,1)S(1)} all-gather(bf16[1,2,1024]{2,1,0:T(2,128)(2,1)S(1)} %bitcast.123), channel_id=1, replica_groups=mesh['req'=4,'head'=8] {'head'}, dimensions={0}, use_global_device_ids=true | all-gather | bytes 36864 | tf_op jit(solution)/shard_map/all_gather | solution.py:47
  289.0 1.4 convolution_convert_fusion
  290.6 2.9 fusion.2
  293.9 3.4 fusion
  297.2 0.9 convolution_bitcast_fusion
  299.1 50.7 %all-reduce.13.cloned.1.call-done = f32[16,1024]{1,0:T(8,128)} async-done(((f32[16,1024]{1,0:T(8,128)}), f32[16,1024]{1,0:T(8,128)}) %all-reduce.13.cloned.1.call-update) | async-done | bytes 65552
  349.8 0.9 fusion.213
  350.7 0.9 multiply_reduce_fusion.3
  351.6 0.8 add_convert_fusion.1
  352.5 40.2 %all-gather.3 = bf16[32,2,1024]{2,1,0:T(2,128)(2,1)S(1)} all-gather(bf16[1,2,1024]{2,1,0:T(2,128)(2,1)S(1)} %bitcast.124), channel_id=1, replica_groups=mesh['req'=4,'head'=8] {'req','head'}, dimensions={0}, use_global_device_ids=true | all-gather | bytes 135168 | tf_op jit(solution)/shard_map/all_gather | solution.py:95
  392.7 2.1 fusion.16
  394.9 121.3 %all-reduce.15.cloned.1.call-done = f32[64,1024]{1,0:T(8,128)} async-done(((f32[64,1024]{1,0:T(8,128)}), f32[64,1024]{1,0:T(8,128)}) %all-reduce.15.cloned.1.call-update) | async-done | bytes 262160
  516.2 0.9 fusion.214
  517.1 0.9 multiply_reduce_fusion.2
  518.9 39.9 %all-gather.4 = bf16[32,2,1024]{2,1,0:T(2,128)(2,1)S(1)} all-gather(bf16[1,2,1024]{2,1,0:T(2,128)(2,1)S(1)} %fusion.147), channel_id=1, replica_groups=mesh['req'=4,'head'=8] {'req','head'}, dimensions={0}, use_global_device_ids=true | all-gather | bytes 135168 | tf_op jit(solution)/shard_map/all_gather | solution.py:111
  559.5 1.8 fusion.218
  (63 shorter events, 5.8 us)
Async XLA Ops:
  6.5 553.0 %copy-start = (bf16[1536,1024]{1,0:T(8,128)(2,1)S(1)}, bf16[1536,1024]{1,0:T(8,128)(2,1)}, u32[]{:S(2)}) copy-start(bf16[1536,1024]{1,0:T(8,128)(2,1)} %param.25) | copy-start | bytes 9437188
  6.5 104.2 %all-reduce.9.cloned.1.call-start = ((), (), s32[]{:S(2)}) async-start(), calls=%async_computation | async-start | bytes 131072
  54.4 6.7 %copy-start.4 = (bf16[2,2,64,1024]{3,2,1,0:T(8,128)(2,1)S(1)}, bf16[2,2,64,1024]{3,2,1,0:T(8,128)(2,1)}, u32[]{:S(2)}) copy-start(bf16[2,2,64,1024]{3,2,1,0:T(8,128)(2,1)} %param.19) | copy-start | bytes 1572868
  54.4 7.7 %copy-start.1 = (f32[2,2,1024]{2,1,0:T(2,128)S(1)}, f32[2,2,1024]{2,1,0:T(2,128)}, u32[]{:S(2)}) copy-start(f32[2,2,1024]{2,1,0:T(2,128)} %param.23) | copy-start | bytes 49156
  54.4 7.7 %copy-start.2 = (f32[2,2,1024]{2,1,0:T(2,128)S(1)}, f32[2,2,1024]{2,1,0:T(2,128)}, u32[]{:S(2)}) copy-start(f32[2,2,1024]{2,1,0:T(2,128)} %param.24) | copy-start | bytes 49156
  54.4 7.7 %copy-start.3 = (bf16[2,128]{1,0:T(2,128)(2,1)S(1)}, bf16[2,128]{1,0:T(2,128)(2,1)}, u32[]{:S(2)}) copy-start(bf16[2,128]{1,0:T(2,128)(2,1)} %param.21) | copy-start | bytes 1540
  54.4 7.7 %copy-start.7 = (u32[32]{0:T(128)S(1)}, u32[32]{0:T(128)}, u32[]{:S(2)}) copy-start(u32[32]{0:T(128)} %constant.105) | copy-start | bytes 388
  62.0 215.3 %all-reduce.11.cloned.1.call-start = ((), (), s32[]{:S(2)}) async-start(), calls=%async_computation.1 | async-start | bytes 524288
  155.9 193.8 %all-reduce.13.cloned.1.call-start = ((), (), s32[]{:S(2)}) async-start(), calls=%async_computation.2 | async-start | bytes 131072
  290.6 6.6 %copy-start.5 = (bf16[2,2,64,1024]{3,2,1,0:T(8,128)(2,1)S(1)}, bf16[2,2,64,1024]{3,2,1,0:T(8,128)(2,1)}, u32[]{:S(2)}) copy-start(bf16[2,2,64,1024]{3,2,1,0:T(8,128)(2,1)} %param.19) | copy-start | bytes 1572868
  290.6 7.6 %copy-start.6 = (s32[64]{0:T(128)S(1)}, s32[64]{0:T(128)}, u32[]{:S(2)}) copy-start(s32[64]{0:T(128)} %param.15) | copy-start | bytes 772
  298.2 218.0 %all-reduce.15.cloned.1.call-start = ((), (), s32[]{:S(2)}) async-start(), calls=%async_computation.3 | async-start | bytes 524288
Sparse Core Ops, SparseCore 0:
  62.1 48.6 all-reduce.8
  156.0 121.1 all-reduce.10
  298.3 51.4 all-reduce.12
  395.0 121.1 all-reduce.14
where the time goes:
time: 569 us; the launch traced here: 568 us
  waiting for transfers between devices  341 us (60%)
  blocking collectives  173 us (30%)
  matrix products  23.4 us (4%)
  between operations  14 us (2%)
  other arithmetic  13.4 us (2%)
    unnamed x8, waiting for transfers between devices  341 us
    all_gather x2, blocking collectives, body(): lax.all_gather(normed, ('req', 'head'), axis=0, tiled=True)  80.5 us
    all_gather x1, blocking collectives, body(): gathered = lax.all_gather(hidden_in, ('req', 'head'), axis=0, tiled=True)  43.9 us
    all_gather x1, blocking collectives, body(): everything = lax.all_gather(own_rows, ('req', 'head'), axis=0, tiled=True)  39.9 us
  transfers between devices with their start and end apart: 4, of which 4 were waited for; matrix products, arithmetic and copies ran while one was open for 0% of the time, Pallas kernels for 0%

commit v1 on v0

--- a/solution.py
+++ b/solution.py
@@ -108,7 +108,15 @@
         own_rows = layer_norm(
             normed.astype(jnp.float32) + mlp_out, norm_gain[layer_idx, 1], norm_bias[layer_idx, 1]
         ).astype(jnp.bfloat16)
-    everything = lax.all_gather(own_rows, ("req", "head"), axis=0, tiled=True)
+    ways, here = (lax.axis_size(("req", "head")), lax.axis_index(("req", "head")))
+    grown, reach = (own_rows, 1)
+    while reach < ways:
+        theirs = lax.ppermute(grown, ("req", "head"), [(d, d ^ reach) for d in range(ways)])
+        mine_first = jnp.concatenate([grown, theirs], axis=0)
+        theirs_first = jnp.concatenate([theirs, grown], axis=0)
+        grown = jnp.where(here & reach == 0, mine_first, theirs_first)
+        reach = 2 * reach
+    everything = grown
     inverse = (
         jnp.zeros_like(request_order)
         .at[request_order]

time: 569 us -> 547 us (0.961)
  blocking collectives: 173 us -> 133 us
  waiting for transfers between devices: 341 us -> 353 us
  starting transfers between devices: 0.13 us -> 6.2 us
    all_gather x1 -> x0, blocking collectives: 39.9 us -> none  [body(): everything = lax.all_gather(own_rows, ('req', 'head'), axis=0, tiled=True)]
    ppermute x0 -> x5, waiting for transfers between devices: none -> 11.1 us  [body(): lax.ppermute(grown, ('req', 'head'), [(d, d ^ reach) for d in range(ways)])]
    ppermute x0 -> x5, starting transfers between devices: none -> 6.07 us  [body(): lax.ppermute(grown, ('req', 'head'), [(d, d ^ reach) for d in range(ways)])]
  transfers between devices with their start and end apart: 4 -> 9, of which waited for: 4 -> 9; matrix products, arithmetic and copies ran while one was open for 0% -> 0% of each run, Pallas kernels for 0% -> 0%
where the time goes in v1:
time: 547 us; the launch traced here: 546 us
  waiting for transfers between devices  353 us (65%)
  blocking collectives  133 us (24%)
  matrix products  23.4 us (4%)
  between operations  14 us (3%)
  other arithmetic  13.5 us (2%)
  starting transfers between devices  6.2 us (1%)
    unnamed x8, waiting for transfers between devices  342 us
    all_gather x2, blocking collectives, body(): lax.all_gather(normed, ('req', 'head'), axis=0, tiled=True)  80.5 us
    all_gather x1, blocking collectives, body(): gathered = lax.all_gather(hidden_in, ('req', 'head'), axis=0, tiled=True)  43.9 us
    ppermute x5, waiting for transfers between devices, body(): lax.ppermute(grown, ('req', 'head'), [(d, d ^ reach) for d in range(ways)])  11.1 us
  transfers between devices with their start and end apart: 9, of which 9 were waited for; matrix products, arithmetic and copies ran while one was open for 0% of the time, Pallas kernels for 0%

profile of v1, /device:TPU:0, one launch (start us, length us, event | category | flops | bytes accessed | tf_op | source)
XLA Modules:
  0.0 546.0 jit_solution(4158055733513005439)
XLA Ops:
  7.4 43.9 %all-gather = bf16[32,2,1024]{2,1,0:T(2,128)(2,1)S(1)} all-gather(bf16[1,2,1024]{2,1,0:T(2,128)(2,1)} %bitcast.132), channel_id=1, replica_groups=mesh['req'=4,'head'=8] {'req','head'}, dimensions={0}, use_global_device_ids=true | all-gather | bytes 135168 | tf_op jit(solution)/shard_map/all_gather | solution.py:37
  52.0 1.5 convolution_convert_fusion.1
  54.4 2.9 fusion.6
  57.7 3.4 fusion.4
  61.0 0.9 convolution_bitcast_fusion.1
  63.4 47.4 %all-reduce.9.cloned.1.call-done = f32[16,1024]{1,0:T(8,128)} async-done(((f32[16,1024]{1,0:T(8,128)}), f32[16,1024]{1,0:T(8,128)}) %all-reduce.9.cloned.1.call-update) | async-done | bytes 65552
  111.7 1.0 multiply_reduce_fusion.5
  113.5 40.2 %all-gather.1 = bf16[32,2,1024]{2,1,0:T(2,128)(2,1)S(1)} all-gather(bf16[1,2,1024]{2,1,0:T(2,128)(2,1)S(1)} %bitcast.123), channel_id=1, replica_groups=mesh['req'=4,'head'=8] {'req','head'}, dimensions={0}, use_global_device_ids=true | all-gather | bytes 135168 | tf_op jit(solution)/shard_map/all_gather | solution.py:95
  153.8 2.1 fusion.20
  156.0 121.3 %all-reduce.11.cloned.1.call-done = f32[64,1024]{1,0:T(8,128)} async-done(((f32[64,1024]{1,0:T(8,128)}), f32[64,1024]{1,0:T(8,128)}) %all-reduce.11.cloned.1.call-update) | async-done | bytes 262160
  278.2 0.9 multiply_reduce_fusion.4
  280.0 9.0 %all-gather.2 = bf16[8,2,1024]{2,1,0:T(2,128)(2,1)S(1)} all-gather(bf16[1,2,1024]{2,1,0:T(2,128)(2,1)S(1)} %bitcast.121), channel_id=1, replica_groups=mesh['req'=4,'head'=8] {'head'}, dimensions={0}, use_global_device_ids=true | all-gather | bytes 36864 | tf_op jit(solution)/shard_map/all_gather | solution.py:47
  289.0 1.4 convolution_convert_fusion
  290.6 2.9 fusion.2
  293.9 3.4 fusion
  297.2 0.9 convolution_bitcast_fusion
  298.2 51.5 %all-reduce.13.cloned.1.call-done = f32[16,1024]{1,0:T(8,128)} async-done(((f32[16,1024]{1,0:T(8,128)}), f32[16,1024]{1,0:T(8,128)}) %all-reduce.13.cloned.1.call-update) | async-done | bytes 65552
  350.7 0.9 multiply_reduce_fusion.3
  352.5 40.2 %all-gather.3 = bf16[32,2,1024]{2,1,0:T(2,128)(2,1)S(1)} all-gather(bf16[1,2,1024]{2,1,0:T(2,128)(2,1)S(1)} %bitcast.122), channel_id=1, replica_groups=mesh['req'=4,'head'=8] {'req','head'}, dimensions={0}, use_global_device_ids=true | all-gather | bytes 135168 | tf_op jit(solution)/shard_map/all_gather | solution.py:95
  392.7 2.1 fusion.16
  394.9 121.3 %all-reduce.15.cloned.1.call-done = f32[64,1024]{1,0:T(8,128)} async-done(((f32[64,1024]{1,0:T(8,128)}), f32[64,1024]{1,0:T(8,128)}) %all-reduce.15.cloned.1.call-update) | async-done | bytes 262160
  517.1 0.9 multiply_reduce_fusion.2
  518.9 1.1 collective-permute-done
  520.1 1.5 collective-permute-start.1
  521.6 2.2 collective-permute-done.1
  523.9 1.5 collective-permute-start.2
  526.2 1.5 collective-permute-done.2
  527.7 1.5 collective-permute-start.3
  529.2 2.5 collective-permute-done.3
  531.7 1.5 collective-permute-start.4
  533.2 3.7 collective-permute-done.4
  537.6 1.8 fusion.217
  (76 shorter events, 12.9 us)
Async XLA Ops:
  6.5 531.1 %copy-start = (bf16[1536,1024]{1,0:T(8,128)(2,1)S(1)}, bf16[1536,1024]{1,0:T(8,128)(2,1)}, u32[]{:S(2)}) copy-start(bf16[1536,1024]{1,0:T(8,128)(2,1)} %param.25) | copy-start | bytes 9437188
  6.5 104.2 %all-reduce.9.cloned.1.call-start = ((), (), s32[]{:S(2)}) async-start(), calls=%async_computation | async-start | bytes 131072
  54.4 6.7 %copy-start.4 = (bf16[2,2,64,1024]{3,2,1,0:T(8,128)(2,1)S(1)}, bf16[2,2,64,1024]{3,2,1,0:T(8,128)(2,1)}, u32[]{:S(2)}) copy-start(bf16[2,2,64,1024]{3,2,1,0:T(8,128)(2,1)} %param.19) | copy-start | bytes 1572868
  54.4 7.7 %copy-start.1 = (f32[2,2,1024]{2,1,0:T(2,128)S(1)}, f32[2,2,1024]{2,1,0:T(2,128)}, u32[]{:S(2)}) copy-start(f32[2,2,1024]{2,1,0:T(2,128)} %param.23) | copy-start | bytes 49156
  54.4 7.7 %copy-start.2 = (f32[2,2,1024]{2,1,0:T(2,128)S(1)}, f32[2,2,1024]{2,1,0:T(2,128)}, u32[]{:S(2)}) copy-start(f32[2,2,1024]{2,1,0:T(2,128)} %param.24) | copy-start | bytes 49156
  54.4 7.7 %copy-start.3 = (bf16[2,128]{1,0:T(2,128)(2,1)S(1)}, bf16[2,128]{1,0:T(2,128)(2,1)}, u32[]{:S(2)}) copy-start(bf16[2,128]{1,0:T(2,128)(2,1)} %param.21) | copy-start | bytes 1540
  54.4 7.7 %copy-start.7 = (u32[32]{0:T(128)S(1)}, u32[32]{0:T(128)}, u32[]{:S(2)}) copy-start(u32[32]{0:T(128)} %constant.111) | copy-start | bytes 388
  62.0 215.3 %all-reduce.11.cloned.1.call-start = ((), (), s32[]{:S(2)}) async-start(), calls=%async_computation.1 | async-start | bytes 524288
  155.9 193.8 %all-reduce.13.cloned.1.call-start = ((), (), s32[]{:S(2)}) async-start(), calls=%async_computation.2 | async-start | bytes 131072
  290.6 6.6 %copy-start.5 = (bf16[2,2,64,1024]{3,2,1,0:T(8,128)(2,1)S(1)}, bf16[2,2,64,1024]{3,2,1,0:T(8,128)(2,1)}, u32[]{:S(2)}) copy-start(bf16[2,2,64,1024]{3,2,1,0:T(8,128)(2,1)} %param.19) | copy-start | bytes 1572868
  293.5 231.9 %copy-start.6 = (s32[64]{0:T(128)S(1)}, s32[64]{0:T(128)}, u32[]{:S(2)}) copy-start(s32[64]{0:T(128)} %param.15) | copy-start | bytes 772
  298.2 218.0 %all-reduce.15.cloned.1.call-start = ((), (), s32[]{:S(2)}) async-start(), calls=%async_computation.3 | async-start | bytes 524288
  518.9 1.2 collective-permute-start
  520.1 3.7 collective-permute-start.1
  523.9 3.8 collective-permute-start.2
  527.7 4.0 collective-permute-start.3
  531.7 5.2 collective-permute-start.4
Sparse Core Ops, SparseCore 0:
  62.1 48.6 all-reduce.8
  156.0 121.1 all-reduce.10
  298.3 51.4 all-reduce.12
  395.0 121.1 all-reduce.14
